TPU v7x, 32 devices: a whole 2x2x4 slice. The times are simulated.
32 devices in a mesh: groups: 2 (over x), seq: 16 (over z, y, core).
Axes of the slice: x: 2, y: 2, z: 4, core: 2. Of those that a mesh axis runs over, the one named last changes fastest.
Arguments:
- x_in: bfloat16 [4096, 4096], P(('groups', 'seq')), parts along dimension 0, may hold values from -6 to 6
- bc_in: bfloat16 [4096, 1024], P(('groups', 'seq')), parts along dimension 0, may hold values from -6 to 6
- z_in: bfloat16 [4096, 4096], P(('groups', 'seq')), parts along dimension 0, may hold values from -6 to 6
- dt_in: bfloat16 [4096, 128], P(('groups', 'seq')), parts along dimension 0, may hold values from -4 to 4
- conv_weight: float32 [4, 5120], replicated, may hold values from -3 to 3
- conv_bias: float32 [5120], replicated, may hold values from -3 to 3
- dt_bias: float32 [128], replicated, may hold values from -4 to -2
- a_log: float32 [128], replicated, may hold values from -11.5 to 0
- d_skip: float32 [128], replicated, may hold values from 0.5 to 1.5
- norm_gain: float32 [4096], replicated, may hold values from 0.5 to 1.5
- conv_cache: bfloat16 [6, 5120], P('groups'), parts along dimension 0, may hold values from -6 to 6
- cache_state: float32 [256, 32, 64], P('groups'), parts along dimension 0, may hold values from -6 to 6
- lengths: int32 [2], P('groups'), parts along dimension 0, may hold values from 1924 to 2048
Outputs:
- mixed: bfloat16 [4096, 4096], P(('groups', 'seq')), parts along dimension 0
- final_state: float32 [256, 32, 64], P(('groups', 'seq')), parts along dimension 0
There are 2 independent parts, one for each index of `groups`. A program takes and returns all parts, laid end to end along the dimension named above; an argument that names none is the same for every part. Nothing has to cross between parts.
All inputs are finite; a program needn't handle non-finite values.
Results may differ from a plain program's by a relative error of at most 0.0085.
Values may be sent and summed in bfloat16 or wider, within the bound.
A program may use at most 64 MiB of HBM per device.

v0:
```python
import jax
import jax.numpy as jnp
from jax import lax
from jax.sharding import PartitionSpec as P

STATE = 64
GROUPS = 8
CONV_W = 4


def shifted(block, axis, distance):
    devices = range(lax.axis_size(axis))
    route = [(i - distance, i) for i in devices if i - distance in devices]
    return lax.ppermute(block, axis, route)


def conv_silu(extended, conv_weight, conv_bias, count):
    total = jnp.zeros((count, extended.shape[1]), jnp.float32) + conv_bias[None, :]
    for offset in range(CONV_W):
        total = (
            total
            + extended[offset : offset + count].astype(jnp.float32) * conv_weight[offset][None, :]
        )
    return jax.nn.silu(total).astype(jnp.bfloat16)


def block_parts(x_block, b_block, c_block, dt_block, decay_rate):
    block_len, head_count, head_dim = x_block.shape
    group_count = b_block.shape[1]
    per_group = head_count // group_count
    cum_rate = jnp.cumsum(dt_block * decay_rate[None, :], axis=0)
    lower_mask = jnp.arange(block_len)[:, None] >= jnp.arange(block_len)[None, :]
    gap_rate = cum_rate.T[:, :, None] - cum_rate.T[:, None, :]
    decay = jnp.exp(jnp.where(lower_mask[None], gap_rate, -1e30))
    c_dot_b = jnp.einsum("tgn,sgn->gts", c_block, b_block, preferred_element_type=jnp.float32)
    decay_grouped = decay.reshape(group_count, per_group, block_len, block_len)
    dt_grouped = dt_block.T.reshape(group_count, per_group, 1, block_len)
    weight = (c_dot_b[:, None] * decay_grouped * dt_grouped).astype(jnp.bfloat16)
    x_grouped = x_block.reshape(block_len, group_count, per_group, head_dim)
    y_diag = jnp.einsum("gkts,sgkp->tgkp", weight, x_grouped, preferred_element_type=jnp.float32)
    y_diag = y_diag.reshape(block_len, head_count, head_dim)
    tail = jnp.exp(cum_rate[-1][None, :] - cum_rate) * dt_block
    tail_grouped = tail.reshape(block_len, group_count, per_group)
    b_weighted = (b_block.astype(jnp.float32)[:, :, None, :] * tail_grouped[:, :, :, None]).astype(
        jnp.bfloat16
    )
    local = jnp.einsum("sgkp,sgkn->gkpn", x_grouped, b_weighted, preferred_element_type=jnp.float32)
    local = local.reshape(head_count, head_dim, b_block.shape[2])
    return (y_diag, cum_rate, local)


def entering_terms(c_block, cum_rate, state):
    block_len, group_count, state_size = c_block.shape
    head_count, head_dim = (state.shape[0], state.shape[1])
    state_grouped = state.reshape(group_count, head_count // group_count, head_dim, state_size)
    product = jnp.einsum(
        "tgn,gkpn->tgkp",
        c_block.astype(jnp.float32),
        state_grouped,
        precision=lax.Precision.HIGHEST,
    )
    return jnp.exp(cum_rate)[:, :, None] * product.reshape(block_len, head_count, head_dim)


def combine(earlier, later):
    return (earlier[0] * later[0], later[0][..., None, None] * earlier[1] + later[1])


def body(
    x_in,
    bc_in,
    z_in,
    dt_in,
    conv_weight,
    conv_bias,
    dt_bias,
    a_log,
    d_skip,
    norm_gain,
    conv_cache,
    cache_state,
    lengths,
):
    tok_rows, inner_width = x_in.shape
    head_count = dt_in.shape[1]
    head_dim = inner_width // head_count
    devices = lax.axis_size("seq")
    seq_index = lax.axis_index("seq")
    rim_rows = CONV_W - 1
    x_rim, bc_rim = shifted((x_in[tok_rows - rim_rows :], bc_in[tok_rows - rim_rows :]), "seq", 1)
    is_first = seq_index == 0
    x_rim = jnp.where(is_first, conv_cache[:, :inner_width], x_rim)
    bc_rim = jnp.where(is_first, conv_cache[:, inner_width:], bc_rim)
    x_conv = conv_silu(
        jnp.concatenate([x_rim, x_in], axis=0),
        conv_weight[:, :inner_width],
        conv_bias[:inner_width],
        tok_rows,
    )
    bc_conv = conv_silu(
        jnp.concatenate([bc_rim, bc_in], axis=0),
        conv_weight[:, inner_width:],
        conv_bias[inner_width:],
        tok_rows,
    )
    decay_rate = -jnp.exp(a_log)
    share = head_count // devices
    x_send = x_conv.reshape(tok_rows, devices, share * head_dim)
    bc_grouped = bc_conv.reshape(tok_rows, 2, GROUPS, STATE).transpose(0, 2, 1, 3)
    bc_send = jnp.repeat(bc_grouped, devices // GROUPS, axis=1).reshape(
        tok_rows, devices, 2 * STATE
    )
    dt_send = dt_in.reshape(tok_rows, devices, share)
    x_heads, bc_heads, dt_heads = (
        lax.all_to_all(x_send, "seq", split_axis=1, concat_axis=0, tiled=True),
        lax.all_to_all(bc_send, "seq", split_axis=1, concat_axis=0, tiled=True),
        lax.all_to_all(dt_send, "seq", split_axis=1, concat_axis=0, tiled=True),
    )
    x_heads = x_heads.reshape(devices, tok_rows, share, head_dim)
    bc_heads = bc_heads.reshape(devices, tok_rows, 2, STATE)
    b_heads = bc_heads[:, :, 0:1, :]
    c_heads = bc_heads[:, :, 1:2, :]
    my_bias = lax.dynamic_slice_in_dim(dt_bias, seq_index * share, share, 0)
    my_rate = lax.dynamic_slice_in_dim(decay_rate, seq_index * share, share, 0)
    my_skip = lax.dynamic_slice_in_dim(d_skip, seq_index * share, share, 0)
    my_cache = lax.dynamic_slice_in_dim(cache_state, seq_index * share, share, 0)
    positions = jnp.arange(devices * tok_rows).reshape(devices, tok_rows)
    live = (positions < lengths[0]).astype(jnp.float32)
    step_size = (
        jax.nn.softplus(dt_heads.reshape(devices, tok_rows, share).astype(jnp.float32) + my_bias)
        * live[:, :, None]
    )
    parts_fn = jax.vmap(block_parts, in_axes=(0, 0, 0, 0, None))
    y_diag, cum_rate, local = parts_fn(x_heads, b_heads, c_heads, step_size, my_rate)
    block_decay = jnp.exp(cum_rate[:, -1, :])
    incl_decay, incl_state = lax.associative_scan(combine, (block_decay, local))
    before_decay = jnp.concatenate([jnp.ones((1, share), jnp.float32), incl_decay[:-1]], axis=0)
    before_state = jnp.concatenate([jnp.zeros_like(local[:1]), incl_state[:-1]], axis=0)
    entering = before_state + before_decay[:, :, None, None] * my_cache[None]
    y_full = (
        y_diag
        + jax.vmap(entering_terms)(c_heads, cum_rate, entering)
        + my_skip[None, None, :, None] * x_heads.astype(jnp.float32)
    )
    y_heads = (y_full * live[:, :, None, None]).astype(jnp.bfloat16)
    y_back = lax.all_to_all(
        y_heads.reshape(devices * tok_rows, 1, share * head_dim),
        "seq",
        split_axis=0,
        concat_axis=1,
        tiled=True,
    )
    y_out = y_back.reshape(tok_rows, inner_width)
    final_state = incl_state[-1] + incl_decay[-1][:, None, None] * my_cache
    gated = y_out.astype(jnp.float32) * jax.nn.silu(z_in.astype(jnp.float32))
    grouped = gated.reshape(tok_rows, GROUPS, inner_width // GROUPS)
    scale = lax.rsqrt(jnp.mean(grouped * grouped, axis=-1, keepdims=True) + 1e-05)
    mixed = (grouped * scale).reshape(tok_rows, inner_width) * norm_gain[None, :]
    return (mixed.astype(jnp.bfloat16), final_state)


def solution(mesh):
    in_specs = (
        P(("groups", "seq"), None),
        P(("groups", "seq"), None),
        P(("groups", "seq"), None),
        P(("groups", "seq"), None),
        P(),
        P(),
        P(),
        P(),
        P(),
        P(),
        P("groups", None),
        P("groups", None, None),
        P("groups"),
    )
    out_specs = (P(("groups", "seq"), None), P(("groups", "seq"), None, None))
    return jax.shard_map(body, mesh=mesh, in_specs=in_specs, out_specs=out_specs, check_vma=False)
```

profile of v0, /device:TPU:15, one launch (start us, length us, event | category | flops | bytes accessed | tf_op | source)
XLA Modules:
  0.0 283.7 jit_solution(17015971120254956565)
XLA Ops:
  0.6 1.6 copy.228
  2.2 6.5 %all-to-all-start.2 = ((bf16[128,16,8]{0,2,1:T(8,128)(2,1)}), bf16[128,16,8]{0,2,1:T(8,128)(2,1)S(1)}, u32[]{:S(2)}, u32[]{:S(2)}) async-start(bf16[128,16,8]{0,2,1:T(8,128)(2,1)} %bitcast.22), calls=%async_computation.2 | async-start | bytes 65536 | tf_op jit(solution)/shard_map/all_to_all | solution.py:117
  8.7 1.5 slice.205
  10.2 3.4 %collective-permute-start = (bf16[3,4096]{1,0:T(4,128)(2,1)}, bf16[3,4096]{1,0:T(4,128)(2,1)}, u32[]{:S(2)}, u32[]{:S(2)}) collective-permute-start(bf16[3,4096]{1,0:T(4,128)(2,1)} %slice.205), channel_id=1, source_target_pairs={{0,1},{1,2},{2,3},{3,4},{4,5},{5,6},{6,7},{7,8},{8,9},{9,10},{10,1... | collective-permute-start | bytes 73736 | tf_op jit(solution)/shard_map/ppermute | solution.py:14
  14.3 0.9 copy.221
  15.2 2.0 collective-permute-start.1
  17.2 1.7 fusion.59
  18.8 1.5 fusion.58
  20.9 1.2 exponential_negate_fusion
  23.8 1.6 copy.219
  25.5 0.8 copy.223
  27.0 0.9 copy.222
  29.7 1.0 broadcast_select_fusion.1
  30.7 2.5 multiply_convert_fusion.7
  33.9 2.1 copy.218
  36.1 1.4 broadcast_select_fusion
  37.4 1.9 broadcast_in_dim.10
  39.3 5.1 %all-to-all-start.1 = ((bf16[128,16,128]{0,2,1:T(8,128)(2,1)}), bf16[128,16,128]{0,2,1:T(8,128)(2,1)S(1)}, u32[]{:S(2)}, u32[]{:S(2)}) async-start(bf16[128,16,128]{0,2,1:T(8,128)(2,1)} %bitcast.14), calls=%async_computation.1 | async-start | bytes 1048576 | tf_op jit(solution)/shard_map/all_to_all | solution.py:116
  44.4 5.7 %multiply_convert_fusion.4 = bf16[128,4096]{0,1:T(8,128)(2,1)} fusion(bf16[128,4096]{0,1:T(8,128)(2,1)S(1)} %copy.219, bf16[3,4096]{0,1:T(8,128)(2,1)S(1)} %broadcast_select_fusion, f32[4096]{0:T(1024)S(1)} %bitcast.153, f32[4096]{0:T(1024)S(1)} %bitcast.154, f32[4096]{0:T(1024)S(1)} %bitcast.155, f32[4096]{0:T(1024)S(1)} %bitcast.152, f32[4096]{0:T(1024)S(1)} %slice-done.3), kind=kLoop, calls=%fused_computation.35 | loop fusion | flops 13631488 | bytes 2203648 | tf_op jit(solution)/shard_map/convert_element_type | solution.py:24
  50.7 23.3 %fusion.61 = f32[16,128,8]{2,0,1:T(8,128)S(1)} fusion(f32[16,128,8]{2,0,1:T(8,128)S(1)} %copy.229), kind=kOutput, calls=%fused_computation.119 | output fusion | flops 2080768 | bytes 131072 | tf_op jit(solution)/shard_map/vmap(jit(cumsum))/reduce_window_sum | solution.py:31
  74.6 0.8 copy-done.8
  75.5 6.0 %all-to-all-start = ((bf16[128,16,256]{0,2,1:T(8,128)(2,1)}), bf16[128,16,256]{0,2,1:T(8,128)(2,1)S(1)}, u32[]{:S(2)}, u32[]{:S(2)}) async-start(bf16[128,16,256]{0,2,1:T(8,128)(2,1)} %bitcast.4), calls=%async_computation | async-start | bytes 2097152 | tf_op jit(solution)/shard_map/all_to_all | solution.py:115
  81.5 0.8 slice_multiply_fusion.3
  83.4 0.8 fusion.60
  85.6 1.0 copy.230
  87.2 1.5 mul.383
  88.7 3.0 %copy.245 = f32[2048,1,256]{2,0,1:T(8,128)} copy(f32[2048,1,256]{0,2,1:T(8,128)} %mul.383) | data formatting | bytes 4194304 | tf_op jit(solution)/shard_map/vmap()/mul | solution.py:62
  91.7 0.8 exponential_multiply_fusion
  92.5 0.8 fusion.38
  93.3 1.3 fusion.36
  94.6 11.7 %all-to-all-done = bf16[128,16,256]{0,2,1:T(8,128)(2,1)S(1)} async-done(((bf16[128,16,256]{0,2,1:T(8,128)(2,1)}), bf16[128,16,256]{0,2,1:T(8,128)(2,1)S(1)}, u32[]{:S(2)}, u32[]{:S(2)}) %all-to-all-start) | async-done | bytes 1048608 | tf_op jit(solution)/shard_map/all_to_all | solution.py:115
  106.3 2.2 fusion.11
  111.1 8.7 %pad.54 = f32[4,8,32,64]{3,2,1,0:T(8,128)} pad(f32[2,8,32,64]{3,2,1,0:T(8,128)} %pad_maximum_fusion.4, f32[]{:T(128)} %constant.17.clone.1), padding=0_1_1x0_0_0x0_0_0x0_0_0 | pad | bytes 393220 | tf_op jit(solution)/shard_map/pad | solution.py:136
  119.8 8.7 %pad.55 = f32[4,8,32,64]{3,2,1,0:T(8,128)} pad(f32[2,8,32,64]{3,2,1,0:T(8,128)} %pad_add_fusion, f32[]{:T(128)} %constant.17.clone.1), padding=1_0_1x0_0_0x0_0_0x0_0_0 | pad | bytes 393220 | tf_op jit(solution)/shard_map/pad | solution.py:136
  128.5 2.1 add.221
  130.6 15.6 %pad.57 = f32[8,8,32,64]{3,2,1,0:T(8,128)} pad(f32[4,8,32,64]{3,2,1,0:T(8,128)} %add.221, f32[]{:T(128)} %constant.17.clone.1), padding=1_0_1x0_0_0x0_0_0x0_0_0 | pad | bytes 786436 | tf_op jit(solution)/shard_map/pad | solution.py:136
  146.3 1.3 fusion.32
  147.6 0.8 pad_maximum_fusion.2
  148.4 15.6 %pad.56 = f32[8,8,32,64]{3,2,1,0:T(8,128)} pad(f32[4,8,32,64]{3,2,1,0:T(8,128)} %pad_maximum_fusion.2, f32[]{:T(128)} %constant.17.clone.1), padding=0_1_1x0_0_0x0_0_0x0_0_0 | pad | bytes 786436 | tf_op jit(solution)/shard_map/pad | solution.py:136
  164.1 2.9 %add.223 = f32[8,8,32,64]{3,2,1,0:T(8,128)} add(f32[8,8,32,64]{3,2,1,0:T(8,128)} %pad.56, f32[8,8,32,64]{3,2,1,0:T(8,128)} %pad.57) | non-fusion elementwise | flops 131072 | bytes 1572864 | tf_op jit(solution)/shard_map/add | solution.py:136
  167.4 20.5 %pad.58 = f32[16,8,32,64]{3,2,1,0:T(8,128)} pad(f32[8,8,32,64]{3,2,1,0:T(8,128)S(1)} %pad_maximum_fusion.1, f32[]{:T(128)} %constant.17.clone.1), padding=0_1_1x0_0_0x0_0_0x0_0_0 | pad | bytes 1572868 | tf_op jit(solution)/shard_map/pad | solution.py:136
  187.9 20.6 %pad.59 = f32[16,8,32,64]{3,2,1,0:T(8,128)} pad(f32[8,8,32,64]{3,2,1,0:T(8,128)S(1)} %copy-done.2, f32[]{:T(128)} %constant.17.clone.1), padding=1_0_1x0_0_0x0_0_0x0_0_0 | pad | bytes 1572868 | tf_op jit(solution)/shard_map/pad | solution.py:136
  208.5 2.6 slice_add_fusion
  211.1 1.4 fusion.24
  212.6 2.6 copy.244
  215.1 6.2 %copy.246 = f32[2048,1,256]{2,0,1:T(8,128)} copy(f32[2048,1,256]{0,1,2:T(1,128)} %bitcast.143) | data formatting | bytes 4194304 | tf_op jit(solution)/shard_map/vmap()/reshape | solution.py:62
  221.3 2.4 fusion.23
  223.7 2.6 copy.232
  226.3 6.1 %copy.247 = f32[2048,1,256]{2,0,1:T(8,128)} copy(f32[2048,1,256]{0,1,2:T(1,128)} %bitcast.144) | data formatting | bytes 4194304 | tf_op jit(solution)/shard_map/vmap()/reshape | solution.py:41
  232.4 1.6 bitcast_convert_fusion
  233.9 3.0 %copy.248 = f32[16,128,1,256]{3,1,0,2:T(8,128)} copy(f32[16,128,1,256]{1,3,0,2:T(8,128)} %bitcast_convert_fusion) | data formatting | bytes 4194304 | tf_op jit(solution)/shard_map/convert_element_type | solution.py:143
  237.0 3.9 %fusion.16 = bf16[2048,1,256]{2,0,1:T(8,128)(2,1)S(1)} fusion(f32[16,128,1,256]{3,1,0,2:T(8,128)} %copy.248, f32[2048,1,256]{2,0,1:T(8,128)} %copy.247, f32[2048,1,256]{2,0,1:T(8,128)} %copy.245, f32[2048,1,256]{2,0,1:T(8,128)} %copy.246, f32[2048]{0:T(1024)S(1)} %copy-done.17, f32[256]{0:T(256)S(1)} %copy-done.20), kind=kLoop, calls=%fused_computation.28 | loop fusion | flops 3145728 | bytes 9446400 | tf_op jit(solution)/shard_map/convert_element_type | solution.py:145
  241.4 1.4 reduce.6
  242.8 1.1 reshape.300
  243.9 4.8 %all-to-all-start.3 = ((bf16[16,2,16384]{2,1,0:T(2,128)(2,1)}), bf16[16,2,16384]{2,1,0:T(2,128)(2,1)S(1)}, u32[]{:S(2)}, u32[]{:S(2)}) async-start(bf16[16,2,16384]{2,1,0:T(2,128)(2,1)} %reshape.300), calls=%async_computation.3 | async-start | bytes 2097152 | tf_op jit(solution)/shard_map/all_to_all | solution.py:146
  248.8 1.3 copy.252
  250.3 20.5 %pad.159 = f32[15,8,32,64]{3,2,1,0:T(8,128)} pad(f32[8,8,32,64]{3,2,1,0:T(8,128)S(1)} %copy-done.2, f32[]{:T(128)} %constant.17.clone.1), padding=0_0_1x0_0_0x0_0_0x0_0_0 | pad | bytes 1507332
  270.8 1.6 bitcast_add_fusion
  272.4 1.2 all-to-all-done.3
  273.6 1.0 reshape.301
  274.9 1.6 convert_bitcast_fusion
  276.5 2.0 copy.251
  279.7 1.7 fusion.13
  281.4 2.3 copy.253
  (137 shorter events, 14.7 us)
Async XLA Ops:
  0.6 22.2 %copy-start = (f32[128,32,64]{0,2,1:T(8,128)S(1)}, f32[128,32,64]{0,2,1:T(8,128)}, u32[]{:S(2)}) copy-start(f32[128,32,64]{0,2,1:T(8,128)} %param.24) | copy-start | bytes 3145732
  2.2 35.2 %all-to-all-start.2 = ((bf16[128,16,8]{0,2,1:T(8,128)(2,1)}), bf16[128,16,8]{0,2,1:T(8,128)(2,1)S(1)}, u32[]{:S(2)}, u32[]{:S(2)}) async-start(bf16[128,16,8]{0,2,1:T(8,128)(2,1)} %bitcast.22), calls=%async_computation.2 | async-start | bytes 65536 | tf_op jit(solution)/shard_map/all_to_all | solution.py:117
  10.2 23.7 %collective-permute-start = (bf16[3,4096]{1,0:T(4,128)(2,1)}, bf16[3,4096]{1,0:T(4,128)(2,1)}, u32[]{:S(2)}, u32[]{:S(2)}) collective-permute-start(bf16[3,4096]{1,0:T(4,128)(2,1)} %slice.205), channel_id=1, source_target_pairs={{0,1},{1,2},{2,3},{3,4},{4,5},{5,6},{6,7},{7,8},{8,9},{9,10},{10,1... | collective-permute-start | bytes 73736 | tf_op jit(solution)/shard_map/ppermute | solution.py:14
  15.2 14.5 %collective-permute-start.1 = (bf16[3,1024]{0,1:T(8,128)(2,1)}, bf16[3,1024]{0,1:T(8,128)(2,1)}, u32[]{:S(2)}, u32[]{:S(2)}) collective-permute-start(bf16[3,1024]{0,1:T(8,128)(2,1)} %copy.221), channel_id=1, source_target_pairs={{0,1},{1,2},{2,3},{3,4},{4,5},{5,6},{6,7},{7,8},{8,9},{9,10},{10,1... | collective-permute-start | bytes 18440 | tf_op jit(solution)/shard_map/ppermute | solution.py:14
  22.8 2.6 copy-start.13
  22.8 3.6 %slice-start.1 = ((bf16[3,5120]{1,0:T(4,128)(2,1)}), bf16[3,4096]{1,0:T(4,128)(2,1)S(1)}, s32[]{:S(2)}) async-start(bf16[3,5120]{1,0:T(4,128)(2,1)} %param.23), calls=%async_computation.5 | async-start | bytes 65536 | tf_op jit(solution)/shard_map/slice | solution.py:92
  23.2 3.1 %copy-start.25 = (f32[128]{0:T(128)S(1)}, f32[128]{0:T(128)}, u32[]{:S(2)}) copy-start(f32[128]{0:T(128)} %param.19) | copy-start | bytes 1540
  23.2 3.2 %copy-start.26 = (f32[128]{0:T(128)S(1)}, f32[128]{0:T(128)}, u32[]{:S(2)}) copy-start(f32[128]{0:T(128)} %exponential_negate_fusion) | copy-start | bytes 1540
  23.2 3.8 %slice-start.2 = ((bf16[3,5120]{1,0:T(4,128)(2,1)}), bf16[3,1024]{1,0:T(4,128)(2,1)S(1)}, s32[]{:S(2)}) async-start(bf16[3,5120]{1,0:T(4,128)(2,1)} %param.23), calls=%async_computation.6 | async-start | bytes 16384 | tf_op jit(solution)/shard_map/slice | solution.py:93
  25.5 5.2 %slice-start.4 = ((f32[5120]{0:T(1024)}), f32[1024]{0:T(1024)S(1)}, s32[]{:S(2)}) async-start(f32[5120]{0:T(1024)} %param.18), calls=%async_computation.8 | async-start | bytes 8192 | tf_op jit(solution)/shard_map/slice | solution.py:103
  26.4 23.7 %copy-start.21 = (f32[8]{0:T(128)}, f32[8]{0:T(128)S(1)}, u32[]{:S(2)}) copy-start(f32[8]{0:T(128)S(1)} %dynamic_slice.12) | copy-start | bytes 100
  36.1 8.4 %slice-start.3 = ((f32[5120]{0:T(1024)}), f32[4096]{0:T(1024)S(1)}, s32[]{:S(2)}) async-start(f32[5120]{0:T(1024)} %param.18), calls=%async_computation.7 | async-start | bytes 32768 | tf_op jit(solution)/shard_map/slice | solution.py:97
  36.1 8.4 %copy-start.14 = (f32[1,4096]{1,0:T(1,128)S(1)}, f32[1,4096]{1,0:T(1,128)}, u32[]{:S(2)}) copy-start(f32[1,4096]{1,0:T(1,128)} %get-tuple-element.25) | copy-start | bytes 49156
  39.3 35.3 %all-to-all-start.1 = ((bf16[128,16,128]{0,2,1:T(8,128)(2,1)}), bf16[128,16,128]{0,2,1:T(8,128)(2,1)S(1)}, u32[]{:S(2)}, u32[]{:S(2)}) async-start(bf16[128,16,128]{0,2,1:T(8,128)(2,1)} %bitcast.14), calls=%async_computation.1 | async-start | bytes 1048576 | tf_op jit(solution)/shard_map/all_to_all | solution.py:116
  74.6 0.9 copy-start.8
  75.5 30.9 %all-to-all-start = ((bf16[128,16,256]{0,2,1:T(8,128)(2,1)}), bf16[128,16,256]{0,2,1:T(8,128)(2,1)S(1)}, u32[]{:S(2)}, u32[]{:S(2)}) async-start(bf16[128,16,256]{0,2,1:T(8,128)(2,1)} %bitcast.4), calls=%async_computation | async-start | bytes 2097152 | tf_op jit(solution)/shard_map/all_to_all | solution.py:115
  88.7 3.0 %copy-start.22 = (f32[8]{0:T(128)S(1)}, f32[8]{0:T(128)}, u32[]{:S(2)}) copy-start(f32[8]{0:T(128)} %copy-done.21) | copy-start | bytes 100
  88.7 3.8 %copy-start.9 = (bf16[128,16,128]{0,2,1:T(8,128)(2,1)S(1)}, bf16[128,16,128]{0,2,1:T(8,128)(2,1)}, u32[]{:S(2)}) copy-start(bf16[128,16,128]{0,2,1:T(8,128)(2,1)} %copy-done.8) | copy-start | bytes 1572868
  108.8 1.6 copy-start.7
  108.8 0.7 copy-start.23
  108.8 1.5 copy-start.24
  128.5 19.1 %slice-start = ((f32[8,8,32,64]{3,2,1,0:T(8,128)}), f32[1,8,32,64]{3,2,1,0:T(8,128)S(1)}, s32[]{:S(2)}) async-start(f32[8,8,32,64]{3,2,1,0:T(8,128)} %copy-done.7), calls=%async_computation.4 | async-start | bytes 262144 | tf_op jit(solution)/shard_map/slice | solution.py:136
  164.1 2.9 %copy-start.5 = (f32[8,8,32,64]{3,2,1,0:T(8,128)S(1)}, f32[8,8,32,64]{3,2,1,0:T(8,128)}, u32[]{:S(2)}) copy-start(f32[8,8,32,64]{3,2,1,0:T(8,128)} %pad.57) | copy-start | bytes 1572868
  164.1 2.9 %copy-start.6 = (f32[8,8,32,64]{3,2,1,0:T(8,128)S(1)}, f32[8,8,32,64]{3,2,1,0:T(8,128)}, u32[]{:S(2)}) copy-start(f32[8,8,32,64]{3,2,1,0:T(8,128)} %pad.56) | copy-start | bytes 1572868
  167.4 20.5 %copy-start.2 = (f32[8,8,32,64]{3,2,1,0:T(8,128)S(1)}, f32[8,8,32,64]{3,2,1,0:T(8,128)}, u32[]{:S(2)}) copy-start(f32[8,8,32,64]{3,2,1,0:T(8,128)} %add.223) | copy-start | bytes 1572868
  208.5 2.6 copy-start.10
  215.1 6.2 %copy-start.11 = (f32[16,128,128]{2,1,0:T(8,128)S(1)}, f32[16,128,128]{2,1,0:T(8,128)}, u32[]{:S(2)}) copy-start(f32[16,128,128]{2,1,0:T(8,128)} %fusion.36) | copy-start | bytes 3145732
  215.1 6.2 %copy-start.15 = (f32[16,8,128]{2,1,0:T(8,128)S(1)}, f32[16,8,128]{2,1,0:T(8,128)}, u32[]{:S(2)}) copy-start(f32[16,8,128]{2,1,0:T(8,128)} %copy.230) | copy-start | bytes 196612
  215.1 6.2 %copy-start.16 = (f32[16,8,128]{2,1,0:T(8,128)S(1)}, f32[16,8,128]{2,1,0:T(8,128)}, u32[]{:S(2)}) copy-start(f32[16,8,128]{2,1,0:T(8,128)} %get-tuple-element.27) | copy-start | bytes 196612
  215.1 6.2 %copy-start.19 = (pred[128,128]{1,0:T(8,128)(4,1)S(1)}, pred[128,128]{1,0:T(8,128)(4,1)}, u32[]{:S(2)}) copy-start(pred[128,128]{1,0:T(8,128)(4,1)} %iota_compare_fusion) | copy-start | bytes 49156
  233.9 3.0 %copy-start.17 = (f32[2048]{0:T(1024)S(1)}, f32[2048]{0:T(1024)}, u32[]{:S(2)}) copy-start(f32[2048]{0:T(1024)} %fusion.52) | copy-start | bytes 24580
  233.9 3.0 %copy-start.20 = (f32[256]{0:T(256)S(1)}, f32[256]{0:T(256)}, u32[]{:S(2)}) copy-start(f32[256]{0:T(256)} %mul.417) | copy-start | bytes 3076
  242.8 6.0 %copy-start.12 = (bf16[128,4096]{1,0:T(8,128)(2,1)S(1)}, bf16[128,4096]{1,0:T(8,128)(2,1)}, u32[]{:S(2)}) copy-start(bf16[128,4096]{1,0:T(8,128)(2,1)} %param.15) | copy-start | bytes 3145732
  243.9 29.7 %all-to-all-start.3 = ((bf16[16,2,16384]{2,1,0:T(2,128)(2,1)}), bf16[16,2,16384]{2,1,0:T(2,128)(2,1)S(1)}, u32[]{:S(2)}, u32[]{:S(2)}) async-start(bf16[16,2,16384]{2,1,0:T(2,128)(2,1)} %reshape.300), calls=%async_computation.3 | async-start | bytes 2097152 | tf_op jit(solution)/shard_map/all_to_all | solution.py:146
  276.5 2.0 copy-start.3
  278.5 1.2 copy-start.4
  278.5 1.2 copy-start.18
  279.7 4.0 %copy-start.1 = (f32[128,32,64]{0,2,1:T(8,128)S(1)}, f32[128,32,64]{0,2,1:T(8,128)}, u32[]{:S(2)}) copy-start(f32[128,32,64]{0,2,1:T(8,128)} %param.24) | copy-start | bytes 3145732
where the time goes:
time: 289 us; the launch traced here: 284 us
  local copies, waits for them, and re-layouts  169 us (58%)
  other arithmetic  64.6 us (22%)
  starting transfers between devices  27.9 us (10%)
  waiting for transfers between devices  13 us (4%)
  matrix products  7.32 us (3%)
    pad x12, local copies, waits for them, and re-layouts, body(): incl_decay, incl_state = lax.associative_scan(combine, (block_decay, local))  90.2 us
    unnamed x64, local copies, waits for them, and re-layouts  32.5 us
    another operation x1, other arithmetic, block_parts(): cum_rate = jnp.cumsum(dt_block * decay_rate[None, :], axis=0)  23.3 us
    all_to_all x1, waiting for transfers between devices, body(): lax.all_to_all(x_send, 'seq', split_axis=1, concat_axis=0, tiled=True)  11.7 us
    add x8, other arithmetic, body(): incl_decay, incl_state = lax.associative_scan(combine, (block_decay, local))  8.5 us
    convert_element_type x2, other arithmetic, conv_silu(): return jax.nn.silu(total).astype(jnp.bfloat16)  8.19 us
    all_to_all x1, starting transfers between devices, body(): lax.all_to_all(dt_send, 'seq', split_axis=1, concat_axis=0, tiled=True)  6.52 us
    reshape x1, local copies, waits for them, and re-layouts, entering_terms(): product.reshape(block_len, head_count, head_dim)  6.16 us
  transfers between devices with their start and end apart: 6, of which 2 were waited for; matrix products, arithmetic and copies ran while one was open for 31% of the time, Pallas kernels for 0%

commit v1 on v0

v1 whole, which is shorter than its diff:
```python
import functools

import jax
import jax.numpy as jnp
from jax import lax
from jax.experimental import pallas as pl
from jax.experimental.pallas import tpu as pltpu
from jax.sharding import PartitionSpec as P

GROUPS = 8
MESH = pl.DeviceIdType.MESH
F32 = jnp.float32
BF16 = jnp.bfloat16
HIGHEST = lax.Precision.HIGHEST


def iota(shape, dim):
    return lax.broadcasted_iota(jnp.int32, shape, dim)


def split_bf16(value):
    high = value.astype(BF16)
    return high, (value - high.astype(F32)).astype(BF16)


def kernel(
    devices,
    len_ref,
    x_ref,
    bc_ref,
    z_ref,
    dt_ref,
    cw_ref,
    cb_ref,
    head_ref,
    skip_ref,
    gain_ref,
    ccache_ref,
    cstate_ref,
    out_ref,
    final_ref,
    ext,
    xc,
    bt,
    cs,
    ypart,
    factors,
    rim_send,
    rim_recv,
    cache_buf,
    ends,
    dsend,
    drecv,
    dec,
    dmine,
    local,
    pbuf,
    asend,
    abuf,
    esend,
    ebuf,
    psend,
    enter,
    rim_sem,
    cache_sem,
    end_sem,
    d_sems,
    p_sem,
    a_sems,
    e_sems,
    n_sems,
):
    tok, inner = x_ref.shape
    heads = dt_ref.shape[1]
    head_dim = inner // heads
    state = bt.shape[1]
    width = inner // GROUPS
    per_group = heads // GROUPS
    chips = devices // 2
    share = heads // devices
    own = share * head_dim
    half = tok // 2
    owners = per_group // share
    rim_rows = ccache_ref.shape[0]
    pad = ext.shape[0] - tok

    me = lax.axis_index("seq")
    core = lax.rem(me, 2)
    chip = me // 2
    partner = chip * 2 + 1 - core
    after = lax.rem(me + 1, devices)
    before = lax.rem(me + devices - 1, devices)
    far = lax.rem(me + devices + 2 * core - 1, devices)
    even = core == 0

    def remote(src, dst, send, recv, where):
        return pltpu.make_async_remote_copy(
            src_ref=src,
            dst_ref=dst,
            send_sem=send,
            recv_sem=recv,
            device_id={"seq": where},
            device_id_type=MESH,
        )

    def peer_of(d):
        other = lax.rem(chip + d, chips)
        return other, other * 2 + core

    cache_copy = pltpu.make_async_copy(
        cstate_ref.at[pl.ds(pl.multiple_of(me * own, own), own)], cache_buf, cache_sem
    )
    cache_copy.start()

    barrier = pltpu.get_barrier_semaphore()
    for other in (partner, far):
        pl.semaphore_signal(barrier, inc=1, device_id={"seq": other}, device_id_type=MESH)

    def greet(d, carry):
        pl.semaphore_signal(
            barrier, inc=1, device_id={"seq": peer_of(d)[1]}, device_id_type=MESH
        )
        return carry

    lax.fori_loop(1, chips, greet, 0)
    rim_send[:, :inner] = x_ref[tok - rim_rows :, :]
    rim_send[:, inner:] = bc_ref[tok - rim_rows :, :]
    pl.semaphore_wait(barrier, chips + 1)

    rim_copy = remote(rim_send, rim_recv, rim_sem.at[0], rim_sem.at[1], after)
    rim_copy.start()

    live = (iota((tok, 1), 0) + me * tok < len_ref[0]).astype(F32)
    raw = dt_ref[...].astype(F32) + head_ref[0:1, :]
    step = (jnp.maximum(raw, 0.0) + jnp.log1p(jnp.exp(-jnp.abs(raw)))) * live
    rate = -jnp.exp(head_ref[1:2, :]) * step
    lower = (iota((tok, tok), 0) >= iota((tok, tok), 1)).astype(F32)
    cum = jnp.dot(lower, rate, precision=HIGHEST, preferred_element_type=F32)
    end = cum[tok - 1 : tok, :]
    ends[0] = jnp.broadcast_to(end, ends.shape[1:])
    end_copy = remote(ends.at[0], ends.at[1], end_sem.at[0], end_sem.at[1], partner)
    end_copy.start()
    first_mid = cum[half // 2 - 1 : half // 2, :]
    second_mid = cum[half + half // 2 - 1 : half + half // 2, :]
    middle = jnp.where(iota((tok, 1), 0) < half, first_mid, second_mid)
    pieces = (
        jnp.exp(end - cum) * step,
        jnp.exp(cum - middle),
        jnp.exp(middle - cum) * step,
        jnp.exp(cum),
        jnp.exp(second_mid - cum[:half]) * step[:half],
    )
    row = 0
    for piece in pieces:
        high, low = split_bf16(piece)
        factors[row : row + piece.shape[0], :heads] = high
        factors[row : row + piece.shape[0], heads:] = low
        row += piece.shape[0]

    def expand(rows, group):
        hit = lax.rem(iota((2 * heads, width), 0), heads) == (
            group * per_group + iota((2 * heads, width), 1) // head_dim
        )
        return jnp.dot(rows, hit.astype(F32).astype(BF16), preferred_element_type=F32)

    ext[pad:, :inner] = x_ref[...].astype(F32)
    ext[pad:, inner:] = bc_ref[...].astype(F32)

    end_copy.wait()
    pair = ends[0] + ends[1]
    dsend[...] = pair
    drecv[chip] = pair

    def send_decay(d, carry):
        other, where = peer_of(d)
        remote(dsend, drecv.at[chip], d_sems.at[0, other], d_sems.at[1, chip], where).start()
        return carry

    lax.fori_loop(1, chips, send_decay, 0)

    rim_copy.wait()
    first = me == 0
    rim = jnp.where(first, ccache_ref[...].astype(F32), rim_recv[...].astype(F32))
    ext[pad - rim_rows : pad, :] = rim

    def conv(columns):
        total = jnp.broadcast_to(cb_ref[0:1, columns], (tok, columns.size))
        for k in range(rim_rows + 1):
            total = total + ext[pl.ds(pad - rim_rows + k, tok), columns] * cw_ref[k : k + 1, columns]
        return total * jax.nn.sigmoid(total)

    span = GROUPS * state
    b_all = conv(pl.ds(inner, span)).T
    for g in range(GROUPS):
        bt[g] = b_all[g * state : (g + 1) * state].astype(BF16)
    c_all = conv(pl.ds(inner + span, span)).astype(BF16)
    for g in range(GROUPS):
        cs[g] = c_all[:, g * state : (g + 1) * state]

    def columns_of(group):
        return pl.ds(pl.multiple_of(group * width, width), width)

    def local_step(group, carry):
        columns = columns_of(group)
        x = conv(columns).astype(BF16)
        xc[:, columns] = x
        tail = expand(factors[:tok, :], group)
        scaled = (x.astype(F32) * tail).astype(BF16)
        sums = jnp.dot(bt[group], scaled, preferred_element_type=F32).astype(BF16)
        for k in range(owners):
            local[k % 2, group * (owners // 2) + k // 2] = sums[:, k * own : (k + 1) * own]
        return carry

    lax.fori_loop(0, GROUPS, local_step, 0)
    p_copy = remote(local.at[1 - core], pbuf, p_sem.at[0], p_sem.at[1], partner)
    p_copy.start()

    def diag_step(group, carry):
        columns = columns_of(group)
        grown = expand(factors[tok : 3 * tok, :], group)
        grown_off = expand(factors[4 * tok : 4 * tok + half, :], group)
        x = xc[:, columns].astype(F32)
        scaled = (x * grown[tok:]).astype(BF16)
        scaled_off = (x[:half] * grown_off).astype(BF16)
        inner_cb = jnp.dot(cs[group], bt[group], preferred_element_type=F32)
        inner_cb = jnp.where(iota((tok, tok), 0) >= iota((tok, tok), 1), inner_cb, 0.0)
        inner_cb = inner_cb.astype(BF16)
        top = jnp.dot(inner_cb[:half, :half], scaled[:half], preferred_element_type=F32)
        bottom = jnp.dot(
            inner_cb[half:],
            jnp.concatenate([scaled_off, scaled[half:]], axis=0),
            preferred_element_type=F32,
        )
        skip = skip_ref[0:1, columns]
        ypart[:half, columns] = top * grown[:half] + skip * x[:half]
        ypart[half:, columns] = bottom * grown[half:tok] + skip * x[half:]
        return carry

    lax.fori_loop(0, 2, diag_step, 0)

    both = jnp.concatenate([ends[0], ends[1]], axis=0)
    both = jnp.exp(both)

    def widen(o, carry):
        hit = iota((heads, own), 0) == (
            (o * 2 + core) * share + iota((heads, own), 1) // head_dim
        )
        dec[o] = jnp.dot(both, hit.astype(F32), precision=HIGHEST, preferred_element_type=F32)
        return carry

    lax.fori_loop(0, chips, widen, 0)

    def block_decay(o, of_even):
        mine = dec[o, 0:1, :]
        theirs = dec[o, ends.shape[1] : ends.shape[1] + 1, :]
        return jnp.where(even == of_even, mine, theirs)

    def block_local(o, of_even):
        return jnp.where(even == of_even, local[core, o].astype(F32), pbuf[o].astype(F32))

    p_copy.wait()

    def a_copy(other, where):
        return remote(
            asend.at[other], abuf.at[chip], a_sems.at[0, other], a_sems.at[1, chip], where
        )

    def send_pair(d, carry):
        other, where = peer_of(d)
        joined = block_decay(other, False) * block_local(other, True) + block_local(other, False)
        asend[other] = joined.astype(BF16)
        a_copy(other, where).start()
        return carry

    lax.fori_loop(1, chips, send_pair, 0)
    joined = block_decay(chip, False) * block_local(chip, True) + block_local(chip, False)
    abuf[chip] = joined.astype(BF16)

    lax.fori_loop(2, 6, diag_step, 0)

    def wait_decay(d, carry):
        other, where = peer_of(d)
        copy = remote(dsend, drecv.at[other], d_sems.at[0, other], d_sems.at[1, other], where)
        copy.wait()
        return carry

    lax.fori_loop(1, chips, wait_decay, 0)
    hit = iota((heads, own), 0) == (me * share + iota((heads, own), 1) // head_dim)
    dmine[...] = jnp.dot(
        jnp.exp(drecv[:, 0, :]), hit.astype(F32), precision=HIGHEST, preferred_element_type=F32
    )
    cache_copy.wait()

    def wait_pair(d, carry):
        other, where = peer_of(d)
        copy = remote(
            asend.at[other], abuf.at[other], a_sems.at[0, other], a_sems.at[1, other], where
        )
        copy.wait()
        return carry

    lax.fori_loop(1, chips, wait_pair, 0)

    def scan_step(s, carried):
        esend[s] = carried.astype(BF16)
        return dmine[pl.ds(s, 1), :] * carried + abuf[s].astype(F32)

    final = lax.fori_loop(0, chips, scan_step, cache_buf[...].T)

    def send_enter(d, carry):
        other, where = peer_of(d)
        remote(
            esend.at[other], ebuf.at[chip], e_sems.at[0, other], e_sems.at[1, chip], where
        ).start()
        return carry

    lax.fori_loop(1, chips, send_enter, 0)
    final_ref[...] = final.T
    ebuf[chip] = esend[chip]

    lax.fori_loop(6, GROUPS, diag_step, 0)

    def pass_on(o):
        at_even = ebuf[o]
        at_odd = block_decay(o, True) * at_even.astype(F32) + block_local(o, True)
        at_odd = at_odd.astype(BF16)
        enter[core, o] = jnp.where(even, at_even, at_odd)
        psend[o] = jnp.where(even, at_odd, at_even)
        remote(
            psend.at[o], enter.at[core, o], n_sems.at[0, o], n_sems.at[1, o], partner
        ).start()

    pass_on(chip)

    def wait_enter(d, carry):
        other, where = peer_of(d)
        copy = remote(
            esend.at[other], ebuf.at[other], e_sems.at[0, other], e_sems.at[1, other], where
        )
        copy.wait()
        pass_on(other)
        return carry

    lax.fori_loop(1, chips, wait_enter, 0)

    def wait_partner(o, carry):
        remote(
            psend.at[o], enter.at[1 - core, o], n_sems.at[0, o], n_sems.at[1, o], partner
        ).wait()
        return carry

    lax.fori_loop(0, chips, wait_partner, 0)

    def gate_step(group, carry):
        columns = columns_of(group)
        entering = jnp.concatenate(
            [enter[k % 2, group * (owners // 2) + k // 2] for k in range(owners)], axis=1
        )
        carried = expand(factors[3 * tok : 4 * tok, :], group)
        y = ypart[:, columns] + carried * jnp.dot(
            cs[group], entering, preferred_element_type=F32
        )
        y = (y * live).astype(BF16).astype(F32)
        z = z_ref[:, columns].astype(F32)
        gated = y * (z * jax.nn.sigmoid(z))
        scale = lax.rsqrt(jnp.mean(gated * gated, axis=-1, keepdims=True) + 1e-05)
        out_ref[:, columns] = (gated * scale * gain_ref[0:1, columns]).astype(BF16)
        return carry

    lax.fori_loop(0, GROUPS, gate_step, 0)


def body(
    devices,
    x_in,
    bc_in,
    z_in,
    dt_in,
    conv_weight,
    conv_bias,
    dt_bias,
    a_log,
    d_skip,
    norm_gain,
    conv_cache,
    cache_state,
    lengths,
):
    tok, inner = x_in.shape
    wide = inner + bc_in.shape[1]
    heads, head_dim, state = cache_state.shape
    chips = devices // 2
    share = heads // devices
    own = share * head_dim
    rim_rows = conv_cache.shape[0]
    vmem = pl.BlockSpec(memory_space=pltpu.VMEM)
    dma = pltpu.SemaphoreType.DMA
    mixed, final = pl.pallas_call(
        functools.partial(kernel, devices),
        out_shape=(
            jax.ShapeDtypeStruct((tok, inner), BF16),
            jax.ShapeDtypeStruct((own, state), F32),
        ),
        in_specs=[pl.BlockSpec(memory_space=pltpu.SMEM)]
        + [vmem] * 10
        + [pl.BlockSpec(memory_space=pl.ANY)],
        out_specs=(vmem, vmem),
        scratch_shapes=[
            pltpu.VMEM((tok + 8, wide), F32),
            pltpu.VMEM((tok, inner), BF16),
            pltpu.VMEM((GROUPS, state, tok), BF16),
            pltpu.VMEM((GROUPS, tok, state), BF16),
            pltpu.VMEM((tok, inner), F32),
            pltpu.VMEM((4 * tok + tok // 2, 2 * heads), BF16),
            pltpu.VMEM((rim_rows, wide), BF16),
            pltpu.VMEM((rim_rows, wide), BF16),
            pltpu.VMEM((own, state), F32),
            pltpu.VMEM((2, 8, heads), F32),
            pltpu.VMEM((8, heads), F32),
            pltpu.VMEM((chips, 8, heads), F32),
            pltpu.VMEM((chips, 16, own), F32),
            pltpu.VMEM((chips, own), F32),
            pltpu.VMEM((2, chips, state, own), BF16),
            pltpu.VMEM((chips, state, own), BF16),
            pltpu.VMEM((chips, state, own), BF16),
            pltpu.VMEM((chips, state, own), BF16),
            pltpu.VMEM((chips, state, own), BF16),
            pltpu.VMEM((chips, state, own), BF16),
            pltpu.VMEM((chips, state, own), BF16),
            pltpu.VMEM((2, chips, state, own), BF16),
            dma((2,)),
            dma(()),
            dma((2,)),
            dma((2, chips)),
            dma((2,)),
            dma((2, chips)),
            dma((2, chips)),
            dma((2, chips)),
        ],
        compiler_params=pltpu.CompilerParams(
            collective_id=0, has_side_effects=True, vmem_limit_bytes=60 * 1024 * 1024
        ),
    )(
        lengths,
        x_in,
        bc_in,
        z_in,
        dt_in,
        conv_weight,
        conv_bias[None, :],
        jnp.stack([dt_bias, a_log]),
        jnp.repeat(d_skip, head_dim)[None, :],
        norm_gain[None, :],
        conv_cache,
        cache_state.reshape(heads * head_dim, state),
    )
    return mixed, final.reshape(share, head_dim, state)


def solution(mesh):
    tokens = P(("groups", "seq"), None)
    in_specs = (
        tokens,
        tokens,
        tokens,
        tokens,
        P(),
        P(),
        P(),
        P(),
        P(),
        P(),
        P("groups", None),
        P("groups", None, None),
        P("groups"),
    )
    out_specs = (tokens, P(("groups", "seq"), None, None))
    return jax.shard_map(
        functools.partial(body, mesh.shape["seq"]),
        mesh=mesh,
        in_specs=in_specs,
        out_specs=out_specs,
        check_vma=False,
    )
```

time: 289 us -> 45.5 us (0.16)
  the two profiles are of different devices: /device:TPU:15 before, /device:TPU:0 now
where the time goes in v1:
time: 45.5 us; the launch traced here: 45.2 us
  Pallas kernels  34.2 us (75%)
  local copies, waits for them, and re-layouts  8.48 us (19%)
  between operations  1.3 us (3%)
  other arithmetic  1.24 us (3%)
    pallas_call x1, Pallas kernels, body(): pl.pallas_call(functools.partial(kernel, devices), out_shape=(jax.ShapeDt...  34.2 us
    unnamed x5, local copies, waits for them, and re-layouts  7.04 us
    another operation x1, other arithmetic, body(): jnp.stack([dt_bias, a_log])  1.24 us

profile of v1, /device:TPU:0, one launch (start us, length us, event | category | flops | bytes accessed | tf_op | source)
XLA Modules:
  0.0 45.2 jit_solution(15428639227701103208)
XLA Ops:
  1.3 1.2 %pad_maximum_fusion.head_ref = f32[2,128]{1,0:T(2,128)} fusion(f32[1,128]{1,0:T(1,128)} %bitcast.10, f32[1,128]{1,0:T(1,128)} %bitcast.11), kind=kLoop, calls=%fused_computation | loop fusion | flops 256 | bytes 2048 | tf_op jit(solution)/shard_map/stack | solution.py:451
  2.5 0.7 %broadcast_in_dim.10 = f32[128,32]{1,0:T(8,128)S(1)} broadcast(f32[128]{0:T(128)} %param.21), dimensions={0} | broadcast | bytes 16896 | tf_op jit(solution)/shard_map/broadcast_in_dim | solution.py:452
  3.2 0.7 %broadcast_in_dim_reshape.3.skip_ref = f32[1,4096]{1,0:T(1,128)} reshape(f32[128,32]{1,0:T(8,128)S(1)} %broadcast_in_dim.10) | data formatting | bytes 32768 | tf_op jit(solution)/shard_map/broadcast_in_dim;reshape | solution.py:452
  4.0 4.1 %copy.16 = f32[128,32,64]{2,1,0:T(8,128)} copy(f32[128,32,64]{0,2,1:T(8,128)} %param.24) | data formatting | bytes 2097152 | tf_op args[11]
  8.0 34.2 %shard_map.140 = (bf16[128,4096]{1,0:T(8,128)(2,1)}, f32[256,64]{1,0:T(8,128)}) custom-call(s32[1]{0:T(128)S(6)} %copy.19.len_ref, bf16[128,4096]{1,0:T(8,128)(2,1)} %x_ref.1, bf16[128,1024]{1,0:T(8,128)(2,1)} %bc_ref.1, bf16[128,4096]{1,0:T(8,128)(2,1)} %z_ref.1, bf16[128,128]{1,0:T(8,128)(2,1)} %dt_ref.1, f32[4,5120]{1,0:T(4,128)} %cw_ref.1, ...), custom_call_target="tpu_custom_call" | custom-call | tf_op jit(solution)/shard_map/pallas_call | solution.py:398
  42.2 0.0 copy-start
  42.3 2.3 %copy.20 = bf16[128,4096]{1,0:T(8,128)(2,1)} copy(bf16[128,4096]{1,0:T(8,128)(2,1)} %get-tuple-element.8) | data formatting | bytes 2097152
  44.6 0.0 copy-done
  44.6 0.7 %copy.21 = f32[8,32,64]{2,1,0:T(8,128)} copy(f32[8,32,64]{2,1,0:T(8,128)S(1)} %bitcast.7) | data formatting | bytes 131072
Async XLA Ops:
  42.2 2.3 %copy-start = (f32[256,64]{1,0:T(8,128)S(1)}, f32[256,64]{1,0:T(8,128)}, u32[]{:S(2)}) copy-start(f32[256,64]{1,0:T(8,128)} %get-tuple-element.5) | copy-start | bytes 196612

commit v2 on v1

v2 whole, which is shorter than its diff:
```python
import functools

import jax
import jax.numpy as jnp
from jax import lax
from jax.experimental import pallas as pl
from jax.experimental.pallas import tpu as pltpu
from jax.sharding import PartitionSpec as P

GROUPS = 8
MESH = pl.DeviceIdType.MESH
F32 = jnp.float32
BF16 = jnp.bfloat16
HIGHEST = lax.Precision.HIGHEST


def iota(shape, dim):
    return lax.broadcasted_iota(jnp.int32, shape, dim)


def split_bf16(value):
    high = value.astype(BF16)
    return high, (value - high.astype(F32)).astype(BF16)


def sigmoid(value):
    return 0.5 * jnp.tanh(0.5 * value) + 0.5


def kernel(
    devices,
    len_ref,
    x_ref,
    bc_ref,
    z_ref,
    dt_ref,
    cw_ref,
    cb_ref,
    bias_ref,
    log_ref,
    skip_ref,
    gain_ref,
    ccache_ref,
    cstate_ref,
    out_ref,
    final_ref,
    ext,
    xc,
    bt,
    cs,
    ypart,
    zgate,
    carried,
    hits,
    tails,
    factors,
    rim_send,
    rim_recv,
    cache_all,
    cache_buf,
    ends,
    dsend,
    drecv,
    dec,
    dmine,
    local,
    pbuf,
    asend,
    abuf,
    esend,
    ebuf,
    psend,
    enter,
    rim_sem,
    cache_sem,
    end_sem,
    d_sems,
    p_sems,
    a_sems,
    e_sems,
    n_sems,
):
    tok, inner = x_ref.shape
    heads = dt_ref.shape[1]
    head_dim = inner // heads
    state = bt.shape[1]
    width = inner // GROUPS
    per_group = heads // GROUPS
    chips = devices // 2
    share = heads // devices
    own = share * head_dim
    half = tok // 2
    owners = per_group // share
    per_chip = chips // GROUPS
    rim_rows = ccache_ref.shape[0]
    pad = ext.shape[0] - tok

    me = lax.axis_index("seq")
    core = lax.rem(me, 2)
    chip = me // 2
    partner = chip * 2 + 1 - core
    after = lax.rem(me + 1, devices)
    far = lax.rem(me + devices + 2 * core - 1, devices)
    even = core == 0
    home = chip // per_chip

    def remote(src, dst, sems, mine, theirs, where):
        return pltpu.make_async_remote_copy(
            src_ref=src,
            dst_ref=dst,
            send_sem=sems.at[0, mine],
            recv_sem=sems.at[1, theirs],
            device_id={"seq": where},
            device_id_type=MESH,
        )

    def peer_of(d):
        other = lax.rem(chip + d, chips)
        return other, other * 2 + core

    cache_copy = pltpu.make_async_copy(cstate_ref, cache_all, cache_sem)
    cache_copy.start()

    barrier = pltpu.get_barrier_semaphore()
    for other in (partner, far):
        pl.semaphore_signal(barrier, inc=1, device_id={"seq": other}, device_id_type=MESH)

    def greet(d, carry):
        pl.semaphore_signal(
            barrier, inc=1, device_id={"seq": peer_of(d)[1]}, device_id_type=MESH
        )
        return carry

    lax.fori_loop(1, chips, greet, 0)
    rim_send[:, :inner] = x_ref[tok - rim_rows :, :]
    rim_send[:, inner:] = bc_ref[tok - rim_rows :, :]

    live = (iota((tok, 1), 0) + me * tok < len_ref[0]).astype(F32)
    raw = dt_ref[...].astype(F32) + bias_ref[...]
    step = (jnp.maximum(raw, 0.0) + jnp.log1p(jnp.exp(-jnp.abs(raw)))) * live
    rate = -jnp.exp(log_ref[...]) * step
    lower = (iota((tok, tok), 0) >= iota((tok, tok), 1)).astype(F32)
    cum = jnp.dot(lower, rate, precision=HIGHEST, preferred_element_type=F32)
    end = cum[tok - 1 : tok, :]
    ends[0] = jnp.broadcast_to(end, ends.shape[1:])

    pl.semaphore_wait(barrier, chips + 1)
    rim_copy = remote(rim_send, rim_recv, rim_sem, 0, 0, after)
    rim_copy.start()
    end_copy = remote(ends.at[0], ends.at[1], end_sem, 0, 0, partner)
    end_copy.start()

    def keep(ref, row, piece):
        high, low = split_bf16(piece)
        ref[row : row + piece.shape[0], :heads] = high
        ref[row : row + piece.shape[0], heads:] = low

    keep(tails, 0, jnp.exp(end - cum) * step)
    first_mid = cum[half // 2 - 1 : half // 2, :]
    second_mid = cum[half + half // 2 - 1 : half + half // 2, :]
    middle = jnp.where(iota((tok, 1), 0) < half, first_mid, second_mid)
    keep(factors, 0, jnp.exp(cum - middle))
    keep(factors, tok, jnp.exp(middle - cum) * step)
    keep(factors, 2 * tok, jnp.exp(cum))
    keep(factors, 3 * tok, jnp.exp(second_mid - cum[:half]) * step[:half])
    keep(factors, 3 * tok + half, jnp.broadcast_to(skip_ref[...], (16, heads)))

    def columns_of(group):
        return pl.ds(pl.multiple_of(group * width, width), width)

    def build_hits(group, carry):
        hit = lax.rem(iota((2 * heads, width), 0), heads) == (
            group * per_group + iota((2 * heads, width), 1) // head_dim
        )
        hits[:, columns_of(group)] = hit.astype(F32).astype(BF16)
        return carry

    lax.fori_loop(0, GROUPS, build_hits, 0)

    def expand(rows, group):
        return jnp.dot(rows, hits[:, columns_of(group)], preferred_element_type=F32)

    ext[pad:, :inner] = x_ref[...].astype(F32)
    ext[pad:, inner:] = bc_ref[...].astype(F32)

    cache_copy.wait()
    chunk = 8
    column = iota((1, own), 1)
    target = lax.rem(column, head_dim) * heads + me * share + column // head_dim

    def pick(c, total):
        rows = jnp.concatenate([cache_all[c * chunk + i] for i in range(chunk)], axis=1)
        high, low = split_bf16(rows)
        lowest = (rows - high.astype(F32) - low.astype(F32)).astype(BF16)
        hit = iota((chunk * heads, own), 0) + c * chunk * heads == target
        hit = hit.astype(F32).astype(BF16)
        parts = jnp.dot(
            jnp.concatenate([high, low, lowest], axis=0), hit, preferred_element_type=F32
        )
        return total + (parts[:state] + parts[state : 2 * state] + parts[2 * state :])

    cache_buf[...] = lax.fori_loop(
        0, head_dim // chunk, pick, jnp.zeros((state, own), F32)
    )

    end_copy.wait()
    pair = ends[0] + ends[1]
    dsend[...] = pair
    drecv[chip] = pair

    def send_decay(d, carry):
        other, where = peer_of(d)
        remote(dsend, drecv.at[chip], d_sems, other, chip, where).start()
        return carry

    lax.fori_loop(1, chips, send_decay, 0)
    keep(tails, tok, jnp.exp(jnp.concatenate([ends[0], ends[1]], axis=0)))

    rim_copy.wait()
    rim = jnp.where(me == 0, ccache_ref[...].astype(F32), rim_recv[...].astype(F32))
    ext[pad - rim_rows : pad, :] = rim

    def conv(columns):
        total = jnp.broadcast_to(cb_ref[0:1, columns], (tok, columns.size))
        for k in range(rim_rows + 1):
            total = total + ext[pl.ds(pad - rim_rows + k, tok), columns] * cw_ref[k : k + 1, columns]
        return total * sigmoid(total)

    span = GROUPS * state
    b_all = conv(pl.ds(inner, span)).T
    for g in range(GROUPS):
        bt[g] = b_all[g * state : (g + 1) * state].astype(BF16)
    c_all = conv(pl.ds(inner + span, span)).astype(BF16)
    for g in range(GROUPS):
        cs[g] = c_all[:, g * state : (g + 1) * state]

    def p_copy(o):
        return remote(local.at[1 - core, o], pbuf.at[o], p_sems, o, o, partner)

    def a_copy(o):
        return remote(asend.at[o], abuf.at[chip], a_sems, o, chip, o * 2 + core)

    def a_wait(o):
        return remote(asend.at[o], abuf.at[o], a_sems, o, o, o * 2 + core)

    def e_copy(o):
        return remote(esend.at[o], ebuf.at[chip], e_sems, o, chip, o * 2 + core)

    def e_wait(o):
        return remote(esend.at[o], ebuf.at[o], e_sems, o, o, o * 2 + core)

    def n_copy(o):
        return remote(psend.at[o], enter.at[core, o], n_sems, o, o, partner)

    def n_wait(o):
        return remote(psend.at[o], enter.at[1 - core, o], n_sems, o, o, partner)

    def block_decay(o, of_even):
        mine = dec[core, o, 0:1, :]
        theirs = dec[core, o, 8:9, :]
        return jnp.where(even == of_even, mine, theirs)

    def block_local(o, of_even):
        return jnp.where(even == of_even, local[core, o].astype(F32), pbuf[o].astype(F32))

    def group_at(d):
        return lax.rem(home + 1 + d, GROUPS)

    def local_step(d):
        group = group_at(d)
        columns = columns_of(group)
        x = conv(columns).astype(BF16)
        xc[:, columns] = x
        tail = expand(tails[...], group)
        scaled = (x.astype(F32) * tail[:tok]).astype(BF16)
        sums = jnp.dot(bt[group], scaled, preferred_element_type=F32).astype(BF16)
        for k in range(owners):
            o = group * per_chip + k // 2
            local[k % 2, o] = sums[:, k * own : (k + 1) * own]
            dec[k % 2, o] = tail[tok:, k * own : (k + 1) * own]
        for k in range(per_chip):
            p_copy(group * per_chip + k).start()

    def pair_step(d):
        for k in range(per_chip):
            o = group_at(d) * per_chip + k
            p_copy(o).wait_recv()
            joined = block_decay(o, False) * block_local(o, True) + block_local(o, False)
            asend[o] = joined.astype(BF16)

            @pl.when(o != chip)
            def _():
                a_copy(o).start()

            @pl.when(o == chip)
            def _():
                abuf[o] = joined.astype(BF16)

    lag = 2
    for d in range(lag):
        local_step(d)

    def local_pair(d, carry):
        local_step(d)
        pair_step(d - lag)
        return carry

    lax.fori_loop(lag, GROUPS, local_pair, 0)
    for d in range(GROUPS - lag, GROUPS):
        pair_step(d)

    def diag_step(d, carry):
        group = group_at(d)
        columns = columns_of(group)
        grown = expand(factors[...], group)
        x = xc[:, columns].astype(F32)
        scaled = (x * grown[tok : 2 * tok]).astype(BF16)
        scaled_off = (x[:half] * grown[3 * tok : 3 * tok + half]).astype(BF16)
        inner_cb = jnp.dot(cs[group], bt[group], preferred_element_type=F32)
        inner_cb = jnp.where(iota((tok, tok), 0) >= iota((tok, tok), 1), inner_cb, 0.0)
        inner_cb = inner_cb.astype(BF16)
        top = jnp.dot(inner_cb[:half, :half], scaled[:half], preferred_element_type=F32)
        bottom = jnp.dot(
            inner_cb[half:],
            jnp.concatenate([scaled_off, scaled[half:]], axis=0),
            preferred_element_type=F32,
        )
        skip = grown[3 * tok + half : 3 * tok + half + 1]
        ypart[:half, columns] = top * grown[:half] + skip * x[:half]
        ypart[half:, columns] = bottom * grown[half:tok] + skip * x[half:]
        carried[:, columns] = grown[2 * tok : 3 * tok]
        z = z_ref[:, columns].astype(F32)
        zgate[:, columns] = z * sigmoid(z)
        return carry

    split = GROUPS // 2
    lax.fori_loop(0, split, diag_step, 0)

    def wait_decay(d, carry):
        other, where = peer_of(d)
        remote(dsend, drecv.at[other], d_sems, other, other, where).wait()
        return carry

    lax.fori_loop(1, chips, wait_decay, 0)
    hit = iota((heads, own), 0) == (me * share + iota((heads, own), 1) // head_dim)
    dmine[...] = jnp.dot(
        jnp.exp(drecv[:, 0, :]), hit.astype(F32), precision=HIGHEST, preferred_element_type=F32
    )

    def scan_step(s, running):
        esend[s] = running.astype(BF16)

        @pl.when(s != chip)
        def _():
            e_copy(s).start()
            a_wait(s).wait_recv()

        @pl.when(s == chip)
        def _():
            ebuf[s] = running.astype(BF16)

        return dmine[pl.ds(s, 1), :] * running + abuf[s].astype(F32)

    final = lax.fori_loop(0, chips, scan_step, cache_buf[...])
    final_ref[...] = final.T

    lax.fori_loop(split, GROUPS, diag_step, 0)

    def order(d):
        return lax.rem(home + d, GROUPS)

    def pass_step(d):
        for k in range(per_chip):
            o = order(d) * per_chip + k

            @pl.when(o != chip)
            def _():
                e_wait(o).wait_recv()

            at_even = ebuf[o]
            at_odd = block_decay(o, True) * at_even.astype(F32) + block_local(o, True)
            at_odd = at_odd.astype(BF16)
            enter[core, o] = jnp.where(even, at_even, at_odd)
            psend[o] = jnp.where(even, at_odd, at_even)
            n_copy(o).start()

    def gate_step(d):
        group = order(d)
        columns = columns_of(group)
        for k in range(per_chip):
            n_wait(group * per_chip + k).wait_recv()
        entering = jnp.concatenate(
            [enter[k % 2, group * per_chip + k // 2] for k in range(owners)], axis=1
        )
        y = ypart[:, columns] + carried[:, columns] * jnp.dot(
            cs[group], entering, preferred_element_type=F32
        )
        y = (y * live).astype(BF16).astype(F32)
        gated = y * zgate[:, columns]
        scale = lax.rsqrt(jnp.mean(gated * gated, axis=-1, keepdims=True) + 1e-05)
        out_ref[:, columns] = (gated * scale * gain_ref[0:1, columns]).astype(BF16)

    for d in range(lag):
        pass_step(d)

    def pass_gate(d, carry):
        pass_step(d)
        gate_step(d - lag)
        return carry

    lax.fori_loop(lag, GROUPS, pass_gate, 0)
    for d in range(GROUPS - lag, GROUPS):
        gate_step(d)

    def finish(o, carry):
        p_copy(o).wait_send()
        n_copy(o).wait_send()

        @pl.when(o != chip)
        def _():
            a_copy(o).wait_send()
            e_copy(o).wait_send()

        return carry

    lax.fori_loop(0, chips, finish, 0)


def body(
    devices,
    x_in,
    bc_in,
    z_in,
    dt_in,
    conv_weight,
    conv_bias,
    dt_bias,
    a_log,
    d_skip,
    norm_gain,
    conv_cache,
    cache_state,
    lengths,
):
    tok, inner = x_in.shape
    wide = inner + bc_in.shape[1]
    heads, head_dim, state = cache_state.shape
    chips = devices // 2
    share = heads // devices
    own = share * head_dim
    rim_rows = conv_cache.shape[0]
    vmem = pl.BlockSpec(memory_space=pltpu.VMEM)
    dma = pltpu.SemaphoreType.DMA
    states = pltpu.VMEM((chips, state, own), BF16)
    mixed, final = pl.pallas_call(
        functools.partial(kernel, devices),
        out_shape=(
            jax.ShapeDtypeStruct((tok, inner), BF16),
            jax.ShapeDtypeStruct((own, state), F32),
        ),
        in_specs=[pl.BlockSpec(memory_space=pltpu.SMEM)]
        + [vmem] * 11
        + [pl.BlockSpec(memory_space=pl.ANY)],
        out_specs=(vmem, vmem),
        scratch_shapes=[
            pltpu.VMEM((tok + 8, wide), F32),
            pltpu.VMEM((tok, inner), BF16),
            pltpu.VMEM((GROUPS, state, tok), BF16),
            pltpu.VMEM((GROUPS, tok, state), BF16),
            pltpu.VMEM((tok, inner), F32),
            pltpu.VMEM((tok, inner), F32),
            pltpu.VMEM((tok, inner), F32),
            pltpu.VMEM((2 * heads, inner), BF16),
            pltpu.VMEM((tok + 16, 2 * heads), BF16),
            pltpu.VMEM((3 * tok + tok // 2 + 16, 2 * heads), BF16),
            pltpu.VMEM((rim_rows, wide), BF16),
            pltpu.VMEM((rim_rows, wide), BF16),
            pltpu.VMEM((head_dim, state, heads), F32),
            pltpu.VMEM((state, own), F32),
            pltpu.VMEM((2, 8, heads), F32),
            pltpu.VMEM((8, heads), F32),
            pltpu.VMEM((chips, 8, heads), F32),
            pltpu.VMEM((2, chips, 16, own), F32),
            pltpu.VMEM((chips, own), F32),
            pltpu.VMEM((2, chips, state, own), BF16),
            states,
            states,
            states,
            states,
            states,
            states,
            pltpu.VMEM((2, chips, state, own), BF16),
            dma((2, 1)),
            dma(()),
            dma((2, 1)),
        ]
        + [dma((2, chips))] * 5,
        compiler_params=pltpu.CompilerParams(
            collective_id=0, has_side_effects=True, vmem_limit_bytes=60 * 1024 * 1024
        ),
    )(
        lengths,
        x_in,
        bc_in,
        z_in,
        dt_in,
        conv_weight,
        conv_bias[None, :],
        dt_bias[None, :],
        a_log[None, :],
        d_skip[None, :],
        norm_gain[None, :],
        conv_cache,
        jnp.transpose(cache_state, (1, 2, 0)),
    )
    return mixed, final.reshape(share, head_dim, state)


def solution(mesh):
    tokens = P(("groups", "seq"), None)
    in_specs = (
        tokens,
        tokens,
        tokens,
        tokens,
        P(),
        P(),
        P(),
        P(),
        P(),
        P(),
        P("groups", None),
        P("groups", None, None),
        P("groups"),
    )
    out_specs = (tokens, P(("groups", "seq"), None, None))
    return jax.shard_map(
        functools.partial(body, mesh.shape["seq"]),
        mesh=mesh,
        in_specs=in_specs,
        out_specs=out_specs,
        check_vma=False,
    )
```

time: 45.5 us -> 34.1 us (0.75)
  the two profiles are of different devices: /device:TPU:0 before, /device:TPU:15 now
where the time goes in v2:
time: 34.1 us; the launch traced here: 33.9 us
  Pallas kernels  29.6 us (87%)
  local copies, waits for them, and re-layouts  2.98 us (9%)
  between operations  1.3 us (4%)
    pallas_call x1, Pallas kernels, body(): pl.pallas_call(functools.partial(kernel, devices), out_shape=(jax.ShapeDt...  29.6 us
    unnamed x4, local copies, waits for them, and re-layouts  2.98 us

profile of v2, /device:TPU:15, one launch (start us, length us, event | category | flops | bytes accessed | tf_op | source)
XLA Modules:
  0.0 33.9 jit_solution(10130373164904204674)
XLA Ops:
  1.3 29.6 %shard_map.140 = (bf16[128,4096]{1,0:T(8,128)(2,1)}, f32[256,64]{1,0:T(8,128)}) custom-call(s32[1]{0:T(128)S(6)} %copy.17.len_ref, bf16[128,4096]{1,0:T(8,128)(2,1)} %x_ref.1, bf16[128,1024]{1,0:T(8,128)(2,1)} %bc_ref.1, bf16[128,4096]{1,0:T(8,128)(2,1)} %z_ref.1, bf16[128,128]{1,0:T(8,128)(2,1)} %dt_ref.1, f32[4,5120]{1,0:T(4,128)} %cw_ref.1, ...), custom_call_target="tpu_custom_call" | custom-call | tf_op jit(solution)/shard_map/pallas_call | solution.py:455
  30.9 0.0 copy-start
  30.9 2.3 %copy.18 = bf16[128,4096]{1,0:T(8,128)(2,1)} copy(bf16[128,4096]{1,0:T(8,128)(2,1)} %get-tuple-element.8) | data formatting | bytes 2097152
  33.3 0.0 copy-done
  33.3 0.7 %copy.19 = f32[8,32,64]{2,1,0:T(8,128)} copy(f32[8,32,64]{2,1,0:T(8,128)S(1)} %bitcast.8) | data formatting | bytes 131072
Async XLA Ops:
  30.9 2.3 %copy-start = (f32[256,64]{1,0:T(8,128)S(1)}, f32[256,64]{1,0:T(8,128)}, u32[]{:S(2)}) copy-start(f32[256,64]{1,0:T(8,128)} %get-tuple-element.5) | copy-start | bytes 196612

commit v3 on v2

--- a/solution.py
+++ b/solution.py
@@ -30,6 +30,20 @@
 def kernel(
     devices,
     len_ref,
+    x_hbm,
+    bc_hbm,
+    z_hbm,
+    dt_hbm,
+    cw_hbm,
+    cb_hbm,
+    bias_hbm,
+    log_hbm,
+    skip_hbm,
+    gain_hbm,
+    ccache_hbm,
+    cstate_hbm,
+    out_ref,
+    final_ref,
     x_ref,
     bc_ref,
     z_ref,
@@ -41,11 +55,9 @@
     skip_ref,
     gain_ref,
     ccache_ref,
-    cstate_ref,
-    out_ref,
-    final_ref,
     ext,
     xc,
+    bcv,
     bt,
     cs,
     ypart,
@@ -72,7 +84,7 @@
     psend,
     enter,
     rim_sem,
-    cache_sem,
+    in_sems,
     end_sem,
     d_sems,
     p_sems,
@@ -118,8 +130,27 @@
         other = lax.rem(chip + d, chips)
         return other, other * 2 + core
 
-    cache_copy = pltpu.make_async_copy(cstate_ref, cache_all, cache_sem)
-    cache_copy.start()
+    loads = [
+        pltpu.make_async_copy(src, dst, in_sems.at[i])
+        for i, (src, dst) in enumerate(
+            (
+                (dt_hbm, dt_ref),
+                (bias_hbm, bias_ref),
+                (log_hbm, log_ref),
+                (x_hbm, x_ref),
+                (bc_hbm, bc_ref),
+                (cw_hbm, cw_ref),
+                (cb_hbm, cb_ref),
+                (ccache_hbm, ccache_ref),
+                (skip_hbm, skip_ref),
+                (cstate_hbm, cache_all),
+                (z_hbm, z_ref),
+                (gain_hbm, gain_ref),
+            )
+        )
+    ]
+    for load in loads:
+        load.start()
 
     barrier = pltpu.get_barrier_semaphore()
     for other in (partner, far):
@@ -132,8 +163,8 @@
         return carry
 
     lax.fori_loop(1, chips, greet, 0)
-    rim_send[:, :inner] = x_ref[tok - rim_rows :, :]
-    rim_send[:, inner:] = bc_ref[tok - rim_rows :, :]
+    for load in loads[:3]:
+        load.wait()
 
     live = (iota((tok, 1), 0) + me * tok < len_ref[0]).astype(F32)
     raw = dt_ref[...].astype(F32) + bias_ref[...]
@@ -143,6 +174,10 @@
     cum = jnp.dot(lower, rate, precision=HIGHEST, preferred_element_type=F32)
     end = cum[tok - 1 : tok, :]
     ends[0] = jnp.broadcast_to(end, ends.shape[1:])
+    for load in loads[3:5]:
+        load.wait()
+    rim_send[:, :inner] = x_ref[tok - rim_rows :, :]
+    rim_send[:, inner:] = bc_ref[tok - rim_rows :, :]
 
     pl.semaphore_wait(barrier, chips + 1)
     rim_copy = remote(rim_send, rim_recv, rim_sem, 0, 0, after)
@@ -156,52 +191,44 @@
         ref[row : row + piece.shape[0], heads:] = low
 
     keep(tails, 0, jnp.exp(end - cum) * step)
-    first_mid = cum[half // 2 - 1 : half // 2, :]
-    second_mid = cum[half + half // 2 - 1 : half + half // 2, :]
-    middle = jnp.where(iota((tok, 1), 0) < half, first_mid, second_mid)
-    keep(factors, 0, jnp.exp(cum - middle))
-    keep(factors, tok, jnp.exp(middle - cum) * step)
-    keep(factors, 2 * tok, jnp.exp(cum))
-    keep(factors, 3 * tok, jnp.exp(second_mid - cum[:half]) * step[:half])
-    keep(factors, 3 * tok + half, jnp.broadcast_to(skip_ref[...], (16, heads)))
-
     def columns_of(group):
         return pl.ds(pl.multiple_of(group * width, width), width)
 
-    def build_hits(group, carry):
+    def expand(rows, group):
+        return jnp.dot(rows, hits[:, columns_of(group)], preferred_element_type=F32)
+
+    ext[pad:, :inner] = x_ref[...].astype(F32)
+    ext[pad:, inner:] = bc_ref[...].astype(F32)
+
+    for load in loads[5:8]:
+        load.wait()
+
+    def conv(columns, row, rows):
+        total = jnp.broadcast_to(cb_ref[0:1, columns], (rows, columns.size))
+        for k in range(rim_rows + 1):
+            seen = ext[pl.ds(pad - rim_rows + k + row, rows), columns]
+            total = total + seen * cw_ref[k : k + 1, columns]
+        return total * sigmoid(total)
+
+    first = 16
+    chunks = [(first, 16)] + [(row, 32) for row in range(2 * first, tok, 32)]
+
+    def conv_step(group, carry):
+        columns = columns_of(group)
         hit = lax.rem(iota((2 * heads, width), 0), heads) == (
             group * per_group + iota((2 * heads, width), 1) // head_dim
         )
-        hits[:, columns_of(group)] = hit.astype(F32).astype(BF16)
-        return carry
-
-    lax.fori_loop(0, GROUPS, build_hits, 0)
-
-    def expand(rows, group):
-        return jnp.dot(rows, hits[:, columns_of(group)], preferred_element_type=F32)
-
-    ext[pad:, :inner] = x_ref[...].astype(F32)
-    ext[pad:, inner:] = bc_ref[...].astype(F32)
-
-    cache_copy.wait()
-    chunk = 8
-    column = iota((1, own), 1)
-    target = lax.rem(column, head_dim) * heads + me * share + column // head_dim
-
-    def pick(c, total):
-        rows = jnp.concatenate([cache_all[c * chunk + i] for i in range(chunk)], axis=1)
-        high, low = split_bf16(rows)
-        lowest = (rows - high.astype(F32) - low.astype(F32)).astype(BF16)
-        hit = iota((chunk * heads, own), 0) + c * chunk * heads == target
-        hit = hit.astype(F32).astype(BF16)
-        parts = jnp.dot(
-            jnp.concatenate([high, low, lowest], axis=0), hit, preferred_element_type=F32
-        )
-        return total + (parts[:state] + parts[state : 2 * state] + parts[2 * state :])
-
-    cache_buf[...] = lax.fori_loop(
-        0, head_dim // chunk, pick, jnp.zeros((state, own), F32)
-    )
+        hits[:, columns] = hit.astype(F32).astype(BF16)
+        for row, rows in chunks:
+            xc[row : row + rows, columns] = conv(columns, row, rows).astype(BF16)
+        return carry
+
+    lax.fori_loop(0, GROUPS, conv_step, 0)
+    span = GROUPS * state
+    sides = (pl.ds(inner, span), pl.ds(inner + span, span))
+    for side, columns in enumerate(sides):
+        for row, rows in chunks:
+            bcv[side, row : row + rows] = conv(columns, row, rows)
 
     end_copy.wait()
     pair = ends[0] + ends[1]
@@ -220,17 +247,12 @@
     rim = jnp.where(me == 0, ccache_ref[...].astype(F32), rim_recv[...].astype(F32))
     ext[pad - rim_rows : pad, :] = rim
 
-    def conv(columns):
-        total = jnp.broadcast_to(cb_ref[0:1, columns], (tok, columns.size))
-        for k in range(rim_rows + 1):
-            total = total + ext[pl.ds(pad - rim_rows + k, tok), columns] * cw_ref[k : k + 1, columns]
-        return total * sigmoid(total)
-
-    span = GROUPS * state
-    b_all = conv(pl.ds(inner, span)).T
+    for side, columns in enumerate(sides):
+        bcv[side, :first] = conv(columns, 0, first)
+    b_all = bcv[0].T
     for g in range(GROUPS):
         bt[g] = b_all[g * state : (g + 1) * state].astype(BF16)
-    c_all = conv(pl.ds(inner + span, span)).astype(BF16)
+    c_all = bcv[1].astype(BF16)
     for g in range(GROUPS):
         cs[g] = c_all[:, g * state : (g + 1) * state]
 
@@ -269,8 +291,8 @@
     def local_step(d):
         group = group_at(d)
         columns = columns_of(group)
-        x = conv(columns).astype(BF16)
-        xc[:, columns] = x
+        xc[:first, columns] = conv(columns, 0, first).astype(BF16)
+        x = xc[:, columns]
         tail = expand(tails[...], group)
         scaled = (x.astype(F32) * tail[:tok]).astype(BF16)
         sums = jnp.dot(bt[group], scaled, preferred_element_type=F32).astype(BF16)
@@ -308,6 +330,18 @@
     lax.fori_loop(lag, GROUPS, local_pair, 0)
     for d in range(GROUPS - lag, GROUPS):
         pair_step(d)
+
+    for load in loads[8:]:
+        load.wait()
+
+    first_mid = cum[half // 2 - 1 : half // 2, :]
+    second_mid = cum[half + half // 2 - 1 : half + half // 2, :]
+    middle = jnp.where(iota((tok, 1), 0) < half, first_mid, second_mid)
+    keep(factors, 0, jnp.exp(cum - middle))
+    keep(factors, tok, jnp.exp(middle - cum) * step)
+    keep(factors, 2 * tok, jnp.exp(cum))
+    keep(factors, 3 * tok, jnp.exp(second_mid - cum[:half]) * step[:half])
+    keep(factors, 3 * tok + half, jnp.broadcast_to(skip_ref[...], (16, heads)))
 
     def diag_step(d, carry):
         group = group_at(d)
@@ -335,6 +369,25 @@
 
     split = GROUPS // 2
     lax.fori_loop(0, split, diag_step, 0)
+
+    chunk = 8
+    column = iota((1, own), 1)
+    target = lax.rem(column, head_dim) * heads + me * share + column // head_dim
+
+    def pick(c, total):
+        rows = jnp.concatenate([cache_all[c * chunk + i] for i in range(chunk)], axis=1)
+        high, low = split_bf16(rows)
+        lowest = (rows - high.astype(F32) - low.astype(F32)).astype(BF16)
+        hit = iota((chunk * heads, own), 0) + c * chunk * heads == target
+        hit = hit.astype(F32).astype(BF16)
+        parts = jnp.dot(
+            jnp.concatenate([high, low, lowest], axis=0), hit, preferred_element_type=F32
+        )
+        return total + (parts[:state] + parts[state : 2 * state] + parts[2 * state :])
+
+    cache_buf[...] = lax.fori_loop(
+        0, head_dim // chunk, pick, jnp.zeros((state, own), F32)
+    )
 
     def wait_decay(d, carry):
         other, where = peer_of(d)
@@ -452,6 +505,20 @@
     vmem = pl.BlockSpec(memory_space=pltpu.VMEM)
     dma = pltpu.SemaphoreType.DMA
     states = pltpu.VMEM((chips, state, own), BF16)
+    arrays = (
+        x_in,
+        bc_in,
+        z_in,
+        dt_in,
+        conv_weight,
+        conv_bias[None, :],
+        dt_bias[None, :],
+        a_log[None, :],
+        d_skip[None, :],
+        norm_gain[None, :],
+        conv_cache,
+        jnp.transpose(cache_state, (1, 2, 0)),
+    )
     mixed, final = pl.pallas_call(
         functools.partial(kernel, devices),
         out_shape=(
@@ -459,12 +526,13 @@
             jax.ShapeDtypeStruct((own, state), F32),
         ),
         in_specs=[pl.BlockSpec(memory_space=pltpu.SMEM)]
-        + [vmem] * 11
-        + [pl.BlockSpec(memory_space=pl.ANY)],
+        + [pl.BlockSpec(memory_space=pltpu.HBM)] * len(arrays),
         out_specs=(vmem, vmem),
-        scratch_shapes=[
+        scratch_shapes=[pltpu.VMEM(a.shape, a.dtype) for a in arrays[:-1]]
+        + [
             pltpu.VMEM((tok + 8, wide), F32),
             pltpu.VMEM((tok, inner), BF16),
+            pltpu.VMEM((2, tok, GROUPS * state), F32),
             pltpu.VMEM((GROUPS, state, tok), BF16),
             pltpu.VMEM((GROUPS, tok, state), BF16),
             pltpu.VMEM((tok, inner), F32),
@@ -491,28 +559,14 @@
             states,
             pltpu.VMEM((2, chips, state, own), BF16),
             dma((2, 1)),
-            dma(()),
+            dma((len(arrays),)),
             dma((2, 1)),
         ]
         + [dma((2, chips))] * 5,
         compiler_params=pltpu.CompilerParams(
             collective_id=0, has_side_effects=True, vmem_limit_bytes=60 * 1024 * 1024
         ),
-    )(
-        lengths,
-        x_in,
-        bc_in,
-        z_in,
-        dt_in,
-        conv_weight,
-        conv_bias[None, :],
-        dt_bias[None, :],
-        a_log[None, :],
-        d_skip[None, :],
-        norm_gain[None, :],
-        conv_cache,
-        jnp.transpose(cache_state, (1, 2, 0)),
-    )
+    )(lengths, *arrays)
     return mixed, final.reshape(share, head_dim, state)
 
 

time: 34.1 us -> 32.2 us (0.944)
  Pallas kernels: 29.6 us -> 27.8 us
    pallas_call x1, Pallas kernels: 29.6 us -> 27.8 us  [body(): pl.pallas_call(functools.partial(kernel, devices), out_shape=(jax.ShapeDt...]
where the time goes in v3:
time: 32.2 us; the launch traced here: 32 us
  Pallas kernels  27.8 us (86%)
  local copies, waits for them, and re-layouts  2.98 us (9%)
  between operations  1.3 us (4%)
    pallas_call x1, Pallas kernels, body(): pl.pallas_call(functools.partial(kernel, devices), out_shape=(jax.ShapeDt...  27.8 us
    unnamed x4, local copies, waits for them, and re-layouts  2.98 us

profile of v3, /device:TPU:15, one launch (start us, length us, event | category | flops | bytes accessed | tf_op | source)
XLA Modules:
  0.0 32.0 jit_solution(490868959704345977)
XLA Ops:
  1.3 27.8 %shard_map.140 = (bf16[128,4096]{1,0:T(8,128)(2,1)}, f32[256,64]{1,0:T(8,128)}) custom-call(s32[1]{0:T(128)S(6)} %copy.17.len_ref, bf16[128,4096]{1,0:T(8,128)(2,1)} %x_hbm.1, bf16[128,1024]{1,0:T(8,128)(2,1)} %bc_hbm.1, bf16[128,4096]{1,0:T(8,128)(2,1)} %z_hbm.1, bf16[128,128]{1,0:T(8,128)(2,1)} %dt_hbm.1, f32[4,5120]{1,0:T(4,128)} %cw_hbm.1, ...), custom_call_target="tpu_custom_call" | custom-call | tf_op jit(solution)/shard_map/pallas_call | solution.py:522
  29.0 0.0 copy-start
  29.1 2.3 %copy.18 = bf16[128,4096]{1,0:T(8,128)(2,1)} copy(bf16[128,4096]{1,0:T(8,128)(2,1)} %get-tuple-element.8) | data formatting | bytes 2097152
  31.4 0.0 copy-done
  31.4 0.7 %copy.19 = f32[8,32,64]{2,1,0:T(8,128)} copy(f32[8,32,64]{2,1,0:T(8,128)S(1)} %bitcast.8) | data formatting | bytes 131072
Async XLA Ops:
  29.0 2.3 %copy-start = (f32[256,64]{1,0:T(8,128)S(1)}, f32[256,64]{1,0:T(8,128)}, u32[]{:S(2)}) copy-start(f32[256,64]{1,0:T(8,128)} %get-tuple-element.5) | copy-start | bytes 196612

commit v4 on v3

--- a/solution.py
+++ b/solution.py
@@ -519,6 +519,7 @@
         conv_cache,
         jnp.transpose(cache_state, (1, 2, 0)),
     )
+    arrays = tuple(pltpu.with_memory_space_constraint(a, pltpu.HBM) for a in arrays)
     mixed, final = pl.pallas_call(
         functools.partial(kernel, devices),
         out_shape=(
@@ -564,7 +565,7 @@
         ]
         + [dma((2, chips))] * 5,
         compiler_params=pltpu.CompilerParams(
-            collective_id=0, has_side_effects=True, vmem_limit_bytes=60 * 1024 * 1024
+            collective_id=0, has_side_effects=True, vmem_limit_bytes=44 * 1024 * 1024
         ),
     )(lengths, *arrays)
     return mixed, final.reshape(share, head_dim, state)

time: 32.2 us -> 29.8 us (0.925)
  local copies, waits for them, and re-layouts: 2.98 us -> 1.63 us
  Pallas kernels: 27.8 us -> 26.7 us
    unnamed x4 -> x2, local copies, waits for them, and re-layouts: 2.98 us -> 1.63 us
    pallas_call x1, Pallas kernels: 27.8 us -> 26.7 us  [body(): pl.pallas_call(functools.partial(kernel, devices), out_shape=(jax.ShapeDt...]
where the time goes in v4:
time: 29.8 us; the launch traced here: 29.7 us
  Pallas kernels  26.7 us (90%)
  local copies, waits for them, and re-layouts  1.63 us (5%)
  between operations  1.29 us (4%)
    pallas_call x1, Pallas kernels, body(): pl.pallas_call(functools.partial(kernel, devices), out_shape=(jax.ShapeDt...  26.7 us
    unnamed x2, local copies, waits for them, and re-layouts  1.63 us

profile of v4, /device:TPU:15, one launch (start us, length us, event | category | flops | bytes accessed | tf_op | source)
XLA Modules:
  0.0 29.7 jit_solution(17152698482527746526)
XLA Ops:
  1.3 26.7 %shard_map.140 = (bf16[128,4096]{1,0:T(8,128)(2,1)S(1)}, f32[256,64]{1,0:T(8,128)S(1)}) custom-call(s32[1]{0:T(128)S(6)} %copy.17.len_ref, bf16[128,4096]{1,0:T(8,128)(2,1)} %x_hbm.1, bf16[128,1024]{1,0:T(8,128)(2,1)} %bc_hbm.1, bf16[128,4096]{1,0:T(8,128)(2,1)} %z_hbm.1, bf16[128,128]{1,0:T(8,128)(2,1)} %dt_hbm.1, f32[4,5120]{1,0:T(4,128)} %cw_hbm.1, ...), custom_call_target="tpu_custom_call" | custom-call | tf_op jit(solution)/shard_map/pallas_call | solution.py:523
  28.0 1.0 %copy.18 = bf16[128,4096]{1,0:T(8,128)(2,1)} copy(bf16[128,4096]{1,0:T(8,128)(2,1)S(1)} %get-tuple-element.8) | data formatting | bytes 2097152
  29.0 0.7 %copy.19 = f32[8,32,64]{2,1,0:T(8,128)} copy(f32[8,32,64]{2,1,0:T(8,128)S(1)} %bitcast.7) | data formatting | bytes 131072
